TPU v7x, 256 devices: a whole 4x4x8 slice. The times are simulated.
256 devices in a mesh: gz: 8 (over x, core), xy: 32 (over y, z).
Axes of the slice: x: 4, y: 4, z: 8, core: 2. Of those that a mesh axis runs over, the one named last changes fastest.
Arguments:
- x_start: float32 [2, 8, 64, 512, 128], P(None, None, 'gz', 'xy'), may hold values from -6 to 6
- rhs: float32 [2, 8, 64, 512, 128], P(None, None, 'gz', 'xy'), may hold values from -20 to 20
- wave_sq: float32 [64, 512, 128], P('gz', 'xy'), may hold values from 0.3 to 1.5
- damping: float32 [64, 512, 128], P('gz', 'xy'), may hold values from 0.05 to 0.6
- front: float32 [2, 8192, 8192], P(None, ('gz', 'xy')), may hold values from -0.0703125 to 0.0703125
- front_order: int32 [8, 32, 32], P('gz', 'xy'), may hold values from 0 to 31, each once within a row
- pair_count: int32 [8, 32, 32], P('gz'), may hold values from 0 to 3, as said below
- sep_cell: int32 [8, 32, 96], P('gz', 'xy'), may hold values from 0 to 14463, as said below
Outputs:
- solution: float32 [2, 8, 64, 512, 128], P(None, None, 'gz', 'xy')
- new_residual: float32 [2, 8, 64, 512, 128], P(None, None, 'gz', 'xy')
Inputs may be any that keep to these rules, and one draw needn't show every extreme that they name: pair_count[g, o, t] counts the separator cells of brick (g, t) whose front rows belong to owner (g, o). For each g and o exactly one brick has 3, one has 2, 27 have 1 and all others 0, so they sum to 32; which bricks is drawn anew for each owner. `sep_cell`: the 96 entries of one brick are distinct local cell indices of that brick, each on its lowest z plane (z = 0) or its lowest y plane (y = 0). Each row front_order[g, o] is a permutation.
All inputs are finite; a program needn't handle non-finite values.
Results may differ from a plain program's by a relative error of at most 0.00011.
Values sent between devices are 32-bit elements; how exact they have to be, the bound alone decides.
A program may use at most 64 MiB of HBM per device.

v0:
```python
from functools import partial
import jax
import jax.numpy as jnp
from jax import lax
from jax.sharding import PartitionSpec as P


def extended(block, sides, width):
    for axis, dim in sides:
        count = lax.axis_size(axis)
        forward = [(i, i + 1) for i in range(count - 1)]
        backward = [(target, source) for source, target in forward]
        low = lax.ppermute(
            lax.slice_in_dim(block, block.shape[dim] - width, None, axis=dim), axis, forward
        )
        high = lax.ppermute(lax.slice_in_dim(block, 0, width, axis=dim), axis, backward)
        block = jnp.concatenate([low, block, high], axis=dim)
    return block


def apply_operator(padded, wave_sq, damping):
    depth, height, width = wave_sq.shape
    centre = padded[:, :, 1 : depth + 1, 1 : height + 1, 1 : width + 1]
    face_sum = jnp.zeros_like(centre)
    edge_sum = jnp.zeros_like(centre)
    corner_sum = jnp.zeros_like(centre)
    for offset_z in (-1, 0, 1):
        for offset_y in (-1, 0, 1):
            for offset_x in (-1, 0, 1):
                nonzero = abs(offset_z) + abs(offset_y) + abs(offset_x)
                if nonzero == 0:
                    continue
                shifted = padded[
                    :,
                    :,
                    1 + offset_z : 1 + offset_z + depth,
                    1 + offset_y : 1 + offset_y + height,
                    1 + offset_x : 1 + offset_x + width,
                ]
                if nonzero == 1:
                    face_sum = face_sum + shifted
                elif nonzero == 2:
                    edge_sum = edge_sum + shifted
                else:
                    corner_sum = corner_sum + shifted
    negative_laplace = (128.0 * centre - 14.0 * face_sum - 3.0 * edge_sum - corner_sum) / 30.0
    real_part = negative_laplace[0] - wave_sq * (centre[0] - damping * centre[1])
    imag_part = negative_laplace[1] - wave_sq * (centre[1] + damping * centre[0])
    return jnp.stack([real_part, imag_part])


def scale_diagonal(field, wave_sq, damping):
    diag_real = 128.0 / 30.0 - wave_sq
    diag_imag = -wave_sq * damping
    modulus = diag_real * diag_real + diag_imag * diag_imag
    return jnp.stack(
        [
            (field[0] * diag_real + field[1] * diag_imag) / modulus,
            (field[1] * diag_real - field[0] * diag_imag) / modulus,
        ]
    )


def pad_width(field):
    return jnp.pad(field, ((0, 0), (0, 0), (0, 0), (0, 0), (1, 1)))


def extend(field):
    padded = extended(field, (("gz", 2), ("xy", 3)), 1)
    return pad_width(padded)


def local(x_start, rhs, wave_sq, damping, front, front_order, pair_count, sep_cell):
    highest = lax.Precision.HIGHEST
    rhs_count = x_start.shape[1]
    components = 2 * rhs_count
    tiles = pair_count.shape[1]
    rows_own = front_order.shape[2]
    slots = sep_cell.shape[2]
    capacity = slots // tiles
    cell_total = wave_sq.size
    own_index = lax.axis_index("xy")
    residual = rhs - apply_operator(extend(x_start), wave_sq, damping)
    scaled = scale_diagonal(residual, wave_sq, damping)
    counts = pair_count[0]
    offsets = jnp.cumsum(counts, axis=1) - counts
    sep_cells = sep_cell[0, 0]
    slot_ids = jnp.arange(slots, dtype=jnp.int32)
    rank_in = slot_ids % capacity
    owner_of = slot_ids // capacity
    sent_counts = lax.dynamic_index_in_dim(counts, own_index, 1, keepdims=False)
    sent_offsets = lax.dynamic_index_in_dim(offsets, own_index, 1, keepdims=False)
    valid_send = (rank_in < sent_counts[owner_of]).astype(jnp.float32)
    flat_residual = residual.reshape(components, cell_total)
    slot_vals = jnp.take(flat_residual, sep_cells, axis=1) * valid_send[None, :]
    got_counts = lax.dynamic_index_in_dim(counts, own_index, 0, keepdims=False)
    got_offsets = lax.dynamic_index_in_dim(offsets, own_index, 0, keepdims=False)
    entry = got_offsets[owner_of] + rank_in
    valid_got = rank_in < got_counts[owner_of]
    row_ids = jnp.arange(rows_own, dtype=jnp.int32)
    entry_map = (valid_got[:, None] & (entry[:, None] == row_ids[None, :])).astype(jnp.float32)
    order_map = (front_order[0, 0][:, None] == row_ids[None, :]).astype(jnp.float32)
    all_slots = lax.all_gather(slot_vals, "xy", axis=1, tiled=True)
    received = lax.dynamic_index_in_dim(
        all_slots.reshape(components, tiles, tiles, capacity), own_index, 2, keepdims=False
    ).reshape(components, slots)
    by_entry = jnp.dot(received, entry_map, precision=highest, preferred_element_type=jnp.float32)
    owned = jnp.dot(by_entry, order_map, precision=highest, preferred_element_type=jnp.float32)
    front_real = front[0]
    front_imag = front[1]
    product = partial(
        lax.dot_general,
        dimension_numbers=(((1,), (1,)), ((), ())),
        precision=highest,
        preferred_element_type=jnp.float32,
    )
    blank = jnp.zeros((rows_own, rhs_count), jnp.float32)
    part_vals = lax.all_gather(owned, ("gz", "xy"), axis=1, tiled=True)
    vals_real = part_vals[:rhs_count]
    vals_imag = part_vals[rhs_count:]
    new_real = blank + product(front_real, vals_real) - product(front_imag, vals_imag)
    new_imag = blank + product(front_real, vals_imag) + product(front_imag, vals_real)
    solved = jnp.concatenate([new_real.T, new_imag.T], axis=0)
    solved_entry = jnp.dot(
        solved, order_map.T, precision=highest, preferred_element_type=jnp.float32
    )
    owner_rows = lax.all_gather(solved_entry, "xy", axis=1, tiled=True)
    pick = jnp.minimum(owner_of * rows_own + sent_offsets[owner_of] + rank_in, tiles * rows_own - 1)
    returned = jnp.take(owner_rows, pick, axis=1) * valid_send[None, :]
    correction = (
        jnp.zeros((components, cell_total), jnp.float32)
        .at[:, sep_cells]
        .add(returned)
        .reshape(residual.shape)
    )
    direction = scaled + correction
    image = apply_operator(extend(direction), wave_sq, damping)
    num_real = jnp.sum(image[0] * residual[0] + image[1] * residual[1], axis=(1, 2, 3))
    num_imag = jnp.sum(image[0] * residual[1] - image[1] * residual[0], axis=(1, 2, 3))
    den_part = jnp.sum(image[0] * image[0] + image[1] * image[1], axis=(1, 2, 3))
    totals = lax.psum(jnp.stack([num_real, num_imag, den_part]), ("gz", "xy"))
    denom = totals[2] + 1e-06
    alpha_real = (totals[0] / denom)[:, None, None, None]
    alpha_imag = (totals[1] / denom)[:, None, None, None]
    solution = jnp.stack(
        [
            x_start[0] + alpha_real * direction[0] - alpha_imag * direction[1],
            x_start[1] + alpha_real * direction[1] + alpha_imag * direction[0],
        ]
    )
    new_residual = jnp.stack(
        [
            residual[0] - alpha_real * image[0] + alpha_imag * image[1],
            residual[1] - alpha_real * image[1] - alpha_imag * image[0],
        ]
    )
    return (solution, new_residual)


def solution(mesh):
    in_specs = (
        P(None, None, "gz", "xy", None),
        P(None, None, "gz", "xy", None),
        P("gz", "xy", None),
        P("gz", "xy", None),
        P(None, ("gz", "xy"), None),
        P("gz", "xy", None),
        P("gz", None, None),
        P("gz", "xy", None),
    )
    out_specs = (P(None, None, "gz", "xy", None), P(None, None, "gz", "xy", None))
    return jax.shard_map(local, mesh=mesh, in_specs=in_specs, out_specs=out_specs, check_vma=False)
```

profile of v0, /device:TPU:1, one launch (start us, length us, event | category | flops | bytes accessed | tf_op | source)
XLA Modules:
  0.0 355.8 jit_solution(13634245641871823886)
XLA Ops:
  1.8 4.5 %collective-permute-start = (f32[2,8,1,16,128]{4,3,2,1,0:T(8,128)S(1)}, f32[2,8,1,16,128]{4,3,2,1,0:T(8,128)S(1)}, u32[]{:S(2)}, u32[]{:S(2)}) collective-permute-start(f32[2,8,1,16,128]{4,3,2,1,0:T(8,128)S(1)} %get-tuple-element.29), channel_id=1, source_target_pairs={{0,32},{32,64},{64,96},{96,128},{128,160},{160,192},{192,224},{1,3... | collective-permute-start | bytes 393224 | tf_op jit(solution)/shard_map/ppermute | solution.py:13
  19.0 3.5 collective-permute-start.2
  24.0 3.9 %collective-permute-done.3 = f32[2,8,10,1,128]{4,3,2,1,0:T(1,128)S(1)} collective-permute-done((f32[2,8,10,1,128]{4,3,2,1,0:T(1,128)S(1)}, f32[2,8,10,1,128]{4,3,2,1,0:T(1,128)S(1)}, u32[]{:S(2)}, u32[]{:S(2)}) %collective-permute-start.3) | collective-permute-done | bytes 81952 | tf_op jit(solution)/shard_map/ppermute | solution.py:16
  30.3 5.6 %fusion.16 = f32[2,8,8,16,128]{4,3,2,1,0:T(8,128)} fusion(f32[2,8,10,16,128]{4,3,2,1,0:T(8,128)S(1)} %constant_dynamic-update-slice_fusion, f32[2,8,10,1,128]{4,3,2,1,0:T(1,128)} %copy-done.6, f32[2,8,10,1,128]{4,3,2,1,0:T(1,128)} %copy-done.5, f32[2,8,10,18,130]{4,3,2,1,0:T(8,128)S(1)} %select_maximum_fusion.4, ...), kind=kLoop, calls=%fused_computation.45 | loop fusion | flops 9961472 | bytes 22708224 | tf_op jit(solution)/shard_map/div | solution.py:46
  37.8 4.6 %copy.23 = f32[16,16384]{0,1:T(8,128)} copy(f32[16,16384]{1,0:T(8,128)S(1)} %reshape.193) | data formatting | bytes 2097152 | tf_op jit(solution)/shard_map/reshape | solution.py:94
  42.4 4.0 %gather_fusion.1 = f32[96,16]{1,0:T(8,128)S(1)} fusion(f32[16,16384]{0,1:T(8,128)} %copy.23, s32[1024]{0:T(1024)S(1)} %pad_clamp_fusion.1), kind=kCustom, calls=%fused_computation.1 | custom fusion | bytes 12672 | tf_op jit(solution)/shard_map/jit(_take)/gather | solution.py:95
  46.6 40.5 %all-gather = f32[32,96,16]{1,2,0:T(8,128)S(1)} all-gather(f32[1,96,16]{1,2,0:T(8,128)S(1)} %copy.24), channel_id=1, replica_groups=mesh['gz'=8,'xy'=32] {'xy'}, dimensions={0}, use_global_device_ids=true | all-gather | bytes 202752 | tf_op jit(solution)/shard_map/all_gather | solution.py:103
  90.9 81.8 %all-gather.1 = f32[256,32,16]{1,2,0:T(8,128)S(1)} all-gather(f32[1,32,16]{1,2,0:T(8,128)S(1)} %convolution_bitcast_fusion.1), channel_id=1, replica_groups=mesh['gz'=8,'xy'=32] {'gz','xy'}, dimensions={0}, use_global_device_ids=true | all-gather | bytes 526336 | tf_op jit(solution)/shard_map/all_gather | solution.py:118
  174.7 2.5 reshape.256
  177.3 2.3 fusion.40
  179.6 2.2 fusion.38
  183.8 36.2 %all-gather.2 = f32[32,32,16]{1,2,0:T(8,128)S(1)} all-gather(f32[1,32,16]{1,2,0:T(8,128)S(1)} %convolution_bitcast_fusion), channel_id=1, replica_groups=mesh['gz'=8,'xy'=32] {'xy'}, dimensions={0}, use_global_device_ids=true | all-gather | bytes 67584 | tf_op jit(solution)/shard_map/all_gather | solution.py:127
  220.2 5.0 %scatter_custom_fusion = f32[16,16384]{0,1:T(8,128)} fusion(s32[96]{0:T(128)S(1)} %fusion.80, f32[]{:T(128)} %constant.81.clone.1, f32[96]{0:T(128)S(1)} %get-tuple-element.33, f32[]{:T(128)} %constant.96.clone.1, pred[96]{0:T(512)(128)(4,1)S(1)} %compare_and_fusion.1, f32[16,1024]{0,1:T(8,128)S(1)} %bitcast.110, s32[1024]{0:T(1024)S(1)} %pad_clamp_fusion), kind=kCustom, calls=%fused_computation.9 | custom fusion | flops 4608 | bytes 1577992 | tf_op jit(solution)/shard_map/scatter-add | solution.py:133
  225.2 5.1 %copy.30 = f32[16,16384]{1,0:T(8,128)S(1)} copy(f32[16,16384]{0,1:T(8,128)} %scatter_custom_fusion) | data formatting | bytes 2097152 | tf_op jit(solution)/shard_map/scatter-add | solution.py:133
  231.6 15.0 %collective-permute-start.4 = (f32[2,8,1,16,128]{4,3,2,1,0:T(8,128)S(1)}, f32[2,8,1,16,128]{4,3,2,1,0:T(8,128)S(1)}, u32[]{:S(2)}, u32[]{:S(2)}) collective-permute-start(f32[2,8,1,16,128]{4,3,2,1,0:T(8,128)S(1)} %get-tuple-element.26), channel_id=1, source_target_pairs={{0,32},{32,64},{64,96},{96,128},{128,160},{160,192},{192,224},{1,3... | collective-permute-start | bytes 393224 | tf_op jit(solution)/shard_map/ppermute | solution.py:13
  246.6 3.0 collective-permute-start.5
  249.6 3.3 collective-permute-done.5
  253.0 3.0 collective-permute-start.6
  257.5 3.7 %collective-permute-done.7 = f32[2,8,10,1,128]{4,3,2,1,0:T(1,128)S(1)} collective-permute-done((f32[2,8,10,1,128]{4,3,2,1,0:T(1,128)S(1)}, f32[2,8,10,1,128]{4,3,2,1,0:T(1,128)S(1)}, u32[]{:S(2)}, u32[]{:S(2)}) %collective-permute-start.7) | collective-permute-done | bytes 81952 | tf_op jit(solution)/shard_map/ppermute | solution.py:16
  261.2 2.3 maximum_maximum_fusion
  263.5 2.7 select_maximum_fusion
  266.2 6.5 %fusion.30 = f32[2,8,8,16,128]{4,3,2,1,0:T(8,128)} fusion(f32[2,8,10,18,130]{4,3,2,1,0:T(8,128)S(1)} %select_maximum_fusion, f32[2,8,10,17,128]{4,3,2,1,0:T(8,128)} %get-tuple-element.17, f32[2,8,10,17,128]{4,3,2,1,0:T(8,128)} %get-tuple-element.16, f32[2,8,1,16,128]{4,3,2,1,0:T(8,128)S(1)} %collective-permute-done.5, ...), kind=kLoop, calls=%fused_computation.60 | loop fusion | flops 8388608 | bytes 27525120 | tf_op jit(solution)/shard_map/div | solution.py:46
  274.4 77.1 %psum.7 = f32[3,8]{1,0:T(4,128)S(1)} all-reduce(f32[3,8]{1,0:T(4,128)S(1)} %pad_maximum_fusion.12), channel_id=1, replica_groups=mesh['gz'=8,'xy'=32] {'gz','xy'}, use_global_device_ids=true, to_apply=%region_5.6 | all-reduce | flops 24 | bytes 192 | tf_op jit(solution)/shard_map/psum | solution.py:141
  351.5 2.0 multiply_add_fusion
  (87 shorter events, 34.6 us)
Async XLA Ops:
  0.6 18.1 %copy-start = (f32[2,8,8,16,128]{4,3,2,1,0:T(8,128)S(1)}, f32[2,8,8,16,128]{4,3,2,1,0:T(8,128)}, u32[]{:S(2)}) copy-start(f32[2,8,8,16,128]{4,3,2,1,0:T(8,128)} %param.8) | copy-start | bytes 3145732
  0.6 17.3 %copy-start.3 = (f32[8,16,128]{2,1,0:T(8,128)S(1)}, f32[8,16,128]{2,1,0:T(8,128)}, u32[]{:S(2)}) copy-start(f32[8,16,128]{2,1,0:T(8,128)} %param.10) | copy-start | bytes 196612
  0.7 17.3 %copy-start.2 = (f32[8,16,128]{2,1,0:T(8,128)S(1)}, f32[8,16,128]{2,1,0:T(8,128)}, u32[]{:S(2)}) copy-start(f32[8,16,128]{2,1,0:T(8,128)} %param.11) | copy-start | bytes 196612
  1.8 17.0 %collective-permute-start = (f32[2,8,1,16,128]{4,3,2,1,0:T(8,128)S(1)}, f32[2,8,1,16,128]{4,3,2,1,0:T(8,128)S(1)}, u32[]{:S(2)}, u32[]{:S(2)}) collective-permute-start(f32[2,8,1,16,128]{4,3,2,1,0:T(8,128)S(1)} %get-tuple-element.29), channel_id=1, source_target_pairs={{0,32},{32,64},{64,96},{96,128},{128,160},{160,192},{192,224},{1,3... | collective-permute-start | bytes 393224 | tf_op jit(solution)/shard_map/ppermute | solution.py:13
  6.3 12.6 %collective-permute-start.1 = (f32[2,8,1,16,128]{4,3,2,1,0:T(8,128)S(1)}, f32[2,8,1,16,128]{4,3,2,1,0:T(8,128)S(1)}, u32[]{:S(2)}, u32[]{:S(2)}) collective-permute-start(f32[2,8,1,16,128]{4,3,2,1,0:T(8,128)S(1)} %get-tuple-element.28), channel_id=1, source_target_pairs={{32,0},{64,32},{96,64},{128,96},{160,128},{192,160},{224,192},{33,... | collective-permute-start | bytes 393224 | tf_op jit(solution)/shard_map/ppermute | solution.py:16
  19.0 5.0 %collective-permute-start.2 = (f32[2,8,10,1,128]{4,3,2,1,0:T(1,128)S(1)}, f32[2,8,10,1,128]{4,3,2,1,0:T(1,128)S(1)}, u32[]{:S(2)}, u32[]{:S(2)}) collective-permute-start(f32[2,8,10,1,128]{4,3,2,1,0:T(1,128)S(1)} %get-tuple-element.20), channel_id=1, source_target_pairs={{0,1},{1,2},{2,3},{3,4},{4,5},{5,6},{6,7},{7,8},{8,9},{9,10},{10,1... | collective-permute-start | bytes 245768 | tf_op jit(solution)/shard_map/ppermute | solution.py:13
  22.6 5.4 %collective-permute-start.3 = (f32[2,8,10,1,128]{4,3,2,1,0:T(1,128)S(1)}, f32[2,8,10,1,128]{4,3,2,1,0:T(1,128)S(1)}, u32[]{:S(2)}, u32[]{:S(2)}) collective-permute-start(f32[2,8,10,1,128]{4,3,2,1,0:T(1,128)S(1)} %get-tuple-element.21), channel_id=1, source_target_pairs={{1,0},{2,1},{3,2},{4,3},{5,4},{6,5},{7,6},{8,7},{9,8},{10,9},{11,1... | collective-permute-start | bytes 245768 | tf_op jit(solution)/shard_map/ppermute | solution.py:16
  24.0 3.9 %copy-start.5 = (f32[2,8,10,1,128]{4,3,2,1,0:T(1,128)}, f32[2,8,10,1,128]{4,3,2,1,0:T(1,128)S(1)}, u32[]{:S(2)}) copy-start(f32[2,8,10,1,128]{4,3,2,1,0:T(1,128)S(1)} %collective-permute-done.2) | copy-start | bytes 245764
  27.9 0.6 copy-start.6
  35.9 1.5 copy-start.4
  87.8 2.9 copy-start.10
  177.3 4.5 %copy-start.1 = (f32[2,32,8192]{2,1,0:T(8,128)S(1)}, f32[2,32,8192]{2,1,0:T(8,128)}, u32[]{:S(2)}) copy-start(f32[2,32,8192]{2,1,0:T(8,128)} %param.12) | copy-start | bytes 6291460
  230.3 0.9 copy-start.7
  230.3 0.9 copy-start.8
  230.3 0.9 copy-start.9
  231.6 18.0 %collective-permute-start.4 = (f32[2,8,1,16,128]{4,3,2,1,0:T(8,128)S(1)}, f32[2,8,1,16,128]{4,3,2,1,0:T(8,128)S(1)}, u32[]{:S(2)}, u32[]{:S(2)}) collective-permute-start(f32[2,8,1,16,128]{4,3,2,1,0:T(8,128)S(1)} %get-tuple-element.26), channel_id=1, source_target_pairs={{0,32},{32,64},{64,96},{96,128},{128,160},{160,192},{192,224},{1,3... | collective-permute-start | bytes 393224 | tf_op jit(solution)/shard_map/ppermute | solution.py:13
  246.6 6.3 %collective-permute-start.5 = (f32[2,8,1,16,128]{4,3,2,1,0:T(8,128)S(1)}, f32[2,8,1,16,128]{4,3,2,1,0:T(8,128)S(1)}, u32[]{:S(2)}, u32[]{:S(2)}) collective-permute-start(f32[2,8,1,16,128]{4,3,2,1,0:T(8,128)S(1)} %get-tuple-element.27), channel_id=1, source_target_pairs={{32,0},{64,32},{96,64},{128,96},{160,128},{192,160},{224,192},{33,... | collective-permute-start | bytes 393224 | tf_op jit(solution)/shard_map/ppermute | solution.py:16
  253.0 4.5 %collective-permute-start.6 = (f32[2,8,10,1,128]{4,3,2,1,0:T(1,128)S(1)}, f32[2,8,10,1,128]{4,3,2,1,0:T(1,128)S(1)}, u32[]{:S(2)}, u32[]{:S(2)}) collective-permute-start(f32[2,8,10,1,128]{4,3,2,1,0:T(1,128)S(1)} %get-tuple-element.18), channel_id=1, source_target_pairs={{0,1},{1,2},{2,3},{3,4},{4,5},{5,6},{6,7},{7,8},{8,9},{9,10},{10,1... | collective-permute-start | bytes 245768 | tf_op jit(solution)/shard_map/ppermute | solution.py:13
  256.0 5.2 %collective-permute-start.7 = (f32[2,8,10,1,128]{4,3,2,1,0:T(1,128)S(1)}, f32[2,8,10,1,128]{4,3,2,1,0:T(1,128)S(1)}, u32[]{:S(2)}, u32[]{:S(2)}) collective-permute-start(f32[2,8,10,1,128]{4,3,2,1,0:T(1,128)S(1)} %get-tuple-element.19), channel_id=1, source_target_pairs={{1,0},{2,1},{3,2},{4,3},{5,4},{6,5},{7,6},{8,7},{9,8},{10,9},{11,1... | collective-permute-start | bytes 245768 | tf_op jit(solution)/shard_map/ppermute | solution.py:16
where the time goes:
time: 357 us; the launch traced here: 356 us
  blocking collectives  236 us (66%)
  other arithmetic  35.8 us (10%)
  starting transfers between devices  33.7 us (9%)
  local copies, waits for them, and re-layouts  31.7 us (9%)
  waiting for transfers between devices  11 us (3%)
  matrix products  6.99 us (2%)
    all_gather x1, blocking collectives, local(): part_vals = lax.all_gather(owned, ('gz', 'xy'), axis=1, tiled=True)  81.8 us
    psum x1, blocking collectives, local(): totals = lax.psum(jnp.stack([num_real, num_imag, den_part]), ('gz', 'xy'))  77.1 us
    all_gather x1, blocking collectives, local(): all_slots = lax.all_gather(slot_vals, 'xy', axis=1, tiled=True)  40.5 us
    all_gather x1, blocking collectives, local(): owner_rows = lax.all_gather(solved_entry, 'xy', axis=1, tiled=True)  36.2 us
    ppermute x4, starting transfers between devices, extended(): lax.ppermute(lax.slice_in_dim(block, block.shape[dim] - width, None, axis...  26 us
    div x2, other arithmetic, apply_operator(): (128.0 * centre - 14.0 * face_sum - 3.0 * edge_sum - corner_sum) / 30.0  12 us
    ppermute x4, waiting for transfers between devices, extended(): lax.ppermute(lax.slice_in_dim(block, 0, width, axis=dim), axis, backward)  10.9 us
    ppermute x4, starting transfers between devices, extended(): lax.ppermute(lax.slice_in_dim(block, 0, width, axis=dim), axis, backward)  7.72 us
  transfers between devices with their start and end apart: 8, of which 4 were waited for; matrix products, arithmetic and copies ran while one was open for 3% of the time, Pallas kernels for 0%

commit v1 on v0

--- a/solution.py
+++ b/solution.py
@@ -3,6 +3,13 @@
 import jax.numpy as jnp
 from jax import lax
 from jax.sharding import PartitionSpec as P
+
+
+def gather_over(x, name, d):
+    devices = lax.axis_size(name)
+    blocks = jnp.stack([x for _ in range(devices)])
+    blocks = lax.all_to_all(blocks, name, split_axis=0, concat_axis=0)
+    return jnp.concatenate(blocks, axis=d)
 
 
 def extended(block, sides, width):
@@ -115,7 +122,7 @@
         preferred_element_type=jnp.float32,
     )
     blank = jnp.zeros((rows_own, rhs_count), jnp.float32)
-    part_vals = lax.all_gather(owned, ("gz", "xy"), axis=1, tiled=True)
+    part_vals = gather_over(owned, ("gz", "xy"), 1)
     vals_real = part_vals[:rhs_count]
     vals_imag = part_vals[rhs_count:]
     new_real = blank + product(front_real, vals_real) - product(front_imag, vals_imag)

time: 357 us -> 327 us (0.916)
  blocking collectives: 236 us -> 152 us
  starting transfers between devices: 33.7 us -> 56.3 us
  waiting for transfers between devices: 11 us -> 32.4 us
  local copies, waits for them, and re-layouts: 31.7 us -> 39.6 us
    all_gather x1 -> x0, blocking collectives: 81.8 us -> none  [local(): part_vals = lax.all_gather(owned, ('gz', 'xy'), axis=1, tiled=True)]
    all_to_all x0 -> x1, starting transfers between devices: none -> 24.1 us  [gather_over(): blocks = lax.all_to_all(blocks, name, split_axis=0, concat_axis=0)]
    all_to_all x0 -> x1, waiting for transfers between devices: none -> 20.3 us  [gather_over(): blocks = lax.all_to_all(blocks, name, split_axis=0, concat_axis=0)]
    slice x0 -> x5, local copies, waits for them, and re-layouts: none -> 5.26 us  [the longest x3 3.34 us: local(): vals_real = part_vals[:rhs_count]]
    unnamed x30 -> x27, local copies, waits for them, and re-layouts: 5.13 us -> 7.77 us
  transfers between devices with their start and end apart: 8 -> 9, of which waited for: 4 -> 5; matrix products, arithmetic and copies ran while one was open for 3% -> 3% of each run, Pallas kernels for 0% -> 0%
where the time goes in v1:
time: 327 us; the launch traced here: 326 us
  blocking collectives  152 us (46%)
  starting transfers between devices  56.3 us (17%)
  local copies, waits for them, and re-layouts  39.6 us (12%)
  other arithmetic  37.8 us (12%)
  waiting for transfers between devices  32.4 us (10%)
  matrix products  6.99 us (2%)
    psum x1, blocking collectives, local(): totals = lax.psum(jnp.stack([num_real, num_imag, den_part]), ('gz', 'xy'))  76.9 us
    all_gather x1, blocking collectives, local(): all_slots = lax.all_gather(slot_vals, 'xy', axis=1, tiled=True)  40.5 us
    all_gather x1, blocking collectives, local(): owner_rows = lax.all_gather(solved_entry, 'xy', axis=1, tiled=True)  34.7 us
    ppermute x4, starting transfers between devices, extended(): lax.ppermute(lax.slice_in_dim(block, block.shape[dim] - width, None, axis...  25.6 us
    all_to_all x1, starting transfers between devices, gather_over(): blocks = lax.all_to_all(blocks, name, split_axis=0, concat_axis=0)  24.1 us
    all_to_all x1, waiting for transfers between devices, gather_over(): blocks = lax.all_to_all(blocks, name, split_axis=0, concat_axis=0)  20.3 us
    div x2, other arithmetic, apply_operator(): (128.0 * centre - 14.0 * face_sum - 3.0 * edge_sum - corner_sum) / 30.0  12.1 us
    ppermute x4, waiting for transfers between devices, extended(): lax.ppermute(lax.slice_in_dim(block, 0, width, axis=dim), axis, backward)  11.9 us
  transfers between devices with their start and end apart: 9, of which 5 were waited for; matrix products, arithmetic and copies ran while one was open for 3% of the time, Pallas kernels for 0%

profile of v1, /device:TPU:1, one launch (start us, length us, event | category | flops | bytes accessed | tf_op | source)
XLA Modules:
  0.0 326.2 jit_solution(17908235273276215462)
XLA Ops:
  1.7 4.5 %collective-permute-start = (f32[2,8,1,16,128]{4,3,2,1,0:T(8,128)S(1)}, f32[2,8,1,16,128]{4,3,2,1,0:T(8,128)S(1)}, u32[]{:S(2)}, u32[]{:S(2)}) collective-permute-start(f32[2,8,1,16,128]{4,3,2,1,0:T(8,128)S(1)} %get-tuple-element.31), channel_id=1, source_target_pairs={{0,32},{32,64},{64,96},{96,128},{128,160},{160,192},{192,224},{1,3... | collective-permute-start | bytes 393224 | tf_op jit(solution)/shard_map/ppermute | solution.py:20
  18.2 3.5 %collective-permute-start.2 = (f32[2,8,10,1,128]{4,3,2,1,0:T(1,128)S(1)}, f32[2,8,10,1,128]{4,3,2,1,0:T(1,128)S(1)}, u32[]{:S(2)}, u32[]{:S(2)}) collective-permute-start(f32[2,8,10,1,128]{4,3,2,1,0:T(1,128)S(1)} %get-tuple-element.22), channel_id=1, source_target_pairs={{0,1},{1,2},{2,3},{3,4},{4,5},{5,6},{6,7},{7,8},{8,9},{9,10},{10,1... | collective-permute-start | bytes 245768 | tf_op jit(solution)/shard_map/ppermute | solution.py:20
  23.2 3.9 %collective-permute-done.3 = f32[2,8,10,1,128]{4,3,2,1,0:T(1,128)S(1)} collective-permute-done((f32[2,8,10,1,128]{4,3,2,1,0:T(1,128)S(1)}, f32[2,8,10,1,128]{4,3,2,1,0:T(1,128)S(1)}, u32[]{:S(2)}, u32[]{:S(2)}) %collective-permute-start.3) | collective-permute-done | bytes 81952 | tf_op jit(solution)/shard_map/ppermute | solution.py:23
  29.6 5.7 %fusion.16 = f32[2,8,8,16,128]{4,3,2,1,0:T(8,128)} fusion(f32[2,8,10,16,128]{4,3,2,1,0:T(8,128)S(1)} %constant_dynamic-update-slice_fusion, f32[2,8,10,1,128]{4,3,2,1,0:T(1,128)} %copy-done.7, f32[2,8,10,1,128]{4,3,2,1,0:T(1,128)} %copy-done.6, f32[2,8,10,18,130]{4,3,2,1,0:T(8,128)S(1)} %select_maximum_fusion.4, ...), kind=kLoop, calls=%fused_computation.44 | loop fusion | flops 9961472 | bytes 22708224 | tf_op jit(solution)/shard_map/div | solution.py:53
  37.1 4.6 %copy.23 = f32[16,16384]{0,1:T(8,128)} copy(f32[16,16384]{1,0:T(8,128)S(1)} %reshape.201) | data formatting | bytes 2097152 | tf_op jit(solution)/shard_map/reshape | solution.py:101
  41.7 4.0 %gather_fusion.1 = f32[96,16]{1,0:T(8,128)S(1)} fusion(f32[16,16384]{0,1:T(8,128)} %copy.23, s32[1024]{0:T(1024)S(1)} %pad_clamp_fusion.1), kind=kCustom, calls=%fused_computation.1 | custom fusion | bytes 12672 | tf_op jit(solution)/shard_map/jit(_take)/gather | solution.py:102
  45.9 40.5 %all-gather = f32[32,96,16]{1,2,0:T(8,128)S(1)} all-gather(f32[1,96,16]{1,2,0:T(8,128)S(1)} %copy.24), channel_id=1, replica_groups=mesh['gz'=8,'xy'=32] {'xy'}, dimensions={0}, use_global_device_ids=true | all-gather | bytes 202752 | tf_op jit(solution)/shard_map/all_gather | solution.py:110
  91.7 3.1 reshape.278
  94.9 24.1 %all-to-all-start = ((f32[256,1,512]{2,1,0:T(1,128)}), f32[256,1,512]{2,1,0:T(1,128)S(1)}, u32[]{:S(2)}, u32[]{:S(2)}) async-start(f32[256,1,512]{2,1,0:T(1,128)} %reshape.278), calls=%async_computation | async-start | bytes 1048576 | tf_op jit(solution)/shard_map/all_to_all | solution.py:11
  120.0 20.3 %all-to-all-done = f32[256,1,512]{2,1,0:T(1,128)S(1)} async-done(((f32[256,1,512]{2,1,0:T(1,128)}), f32[256,1,512]{2,1,0:T(1,128)S(1)}, u32[]{:S(2)}, u32[]{:S(2)}) %all-to-all-start) | async-done | bytes 524320 | tf_op jit(solution)/shard_map/all_to_all | solution.py:11
  144.6 2.6 fusion.86
  149.8 2.3 fusion.40
  152.1 2.2 fusion.38
  156.4 34.7 %all-gather.1 = f32[32,32,16]{1,2,0:T(8,128)S(1)} all-gather(f32[1,32,16]{1,2,0:T(8,128)S(1)} %convolution_bitcast_fusion), channel_id=1, replica_groups=mesh['gz'=8,'xy'=32] {'xy'}, dimensions={0}, use_global_device_ids=true | all-gather | bytes 67584 | tf_op jit(solution)/shard_map/all_gather | solution.py:134
  191.3 5.0 %scatter_custom_fusion = f32[16,16384]{0,1:T(8,128)} fusion(s32[96]{0:T(128)S(1)} %fusion.77, f32[]{:T(128)} %constant.81.clone.1, f32[96]{0:T(128)S(1)} %get-tuple-element.35, f32[]{:T(128)} %constant.96.clone.1, pred[96]{0:T(512)(128)(4,1)S(1)} %compare_and_fusion.1, f32[16,1024]{0,1:T(8,128)S(1)} %bitcast.107, s32[1024]{0:T(1024)S(1)} %pad_clamp_fusion), kind=kCustom, calls=%fused_computation.9 | custom fusion | flops 4608 | bytes 1577992 | tf_op jit(solution)/shard_map/scatter-add | solution.py:140
  196.3 5.1 %copy.31 = f32[16,16384]{1,0:T(8,128)S(1)} copy(f32[16,16384]{0,1:T(8,128)} %scatter_custom_fusion) | data formatting | bytes 2097152 | tf_op jit(solution)/shard_map/scatter-add | solution.py:140
  202.6 14.5 %collective-permute-start.4 = (f32[2,8,1,16,128]{4,3,2,1,0:T(8,128)S(1)}, f32[2,8,1,16,128]{4,3,2,1,0:T(8,128)S(1)}, u32[]{:S(2)}, u32[]{:S(2)}) collective-permute-start(f32[2,8,1,16,128]{4,3,2,1,0:T(8,128)S(1)} %get-tuple-element.28), channel_id=1, source_target_pairs={{0,32},{32,64},{64,96},{96,128},{128,160},{160,192},{192,224},{1,3... | collective-permute-start | bytes 393224 | tf_op jit(solution)/shard_map/ppermute | solution.py:20
  219.1 4.3 %collective-permute-done.5 = f32[2,8,1,16,128]{4,3,2,1,0:T(8,128)S(1)} collective-permute-done((f32[2,8,1,16,128]{4,3,2,1,0:T(8,128)S(1)}, f32[2,8,1,16,128]{4,3,2,1,0:T(8,128)S(1)}, u32[]{:S(2)}, u32[]{:S(2)}) %collective-permute-start.5) | collective-permute-done | bytes 131104 | tf_op jit(solution)/shard_map/ppermute | solution.py:23
  223.5 3.0 collective-permute-start.6
  228.1 3.7 %collective-permute-done.7 = f32[2,8,10,1,128]{4,3,2,1,0:T(1,128)S(1)} collective-permute-done((f32[2,8,10,1,128]{4,3,2,1,0:T(1,128)S(1)}, f32[2,8,10,1,128]{4,3,2,1,0:T(1,128)S(1)}, u32[]{:S(2)}, u32[]{:S(2)}) %collective-permute-start.7) | collective-permute-done | bytes 81952 | tf_op jit(solution)/shard_map/ppermute | solution.py:23
  231.8 2.3 maximum_maximum_fusion
  234.0 2.7 select_maximum_fusion
  236.7 6.4 %fusion.30 = f32[2,8,8,16,128]{4,3,2,1,0:T(8,128)} fusion(f32[2,8,10,18,130]{4,3,2,1,0:T(8,128)S(1)} %select_maximum_fusion, f32[2,8,10,17,128]{4,3,2,1,0:T(8,128)} %get-tuple-element.19, f32[2,8,10,17,128]{4,3,2,1,0:T(8,128)} %get-tuple-element.18, f32[2,8,1,16,128]{4,3,2,1,0:T(8,128)S(1)} %collective-permute-done.5, ...), kind=kLoop, calls=%fused_computation.59 | loop fusion | flops 8388608 | bytes 27525120 | tf_op jit(solution)/shard_map/div | solution.py:53
  245.0 76.9 %psum.7 = f32[3,8]{1,0:T(4,128)S(1)} all-reduce(f32[3,8]{1,0:T(4,128)S(1)} %pad_maximum_fusion.12), channel_id=1, replica_groups=mesh['gz'=8,'xy'=32] {'gz','xy'}, use_global_device_ids=true, to_apply=%region_5.6 | all-reduce | flops 24 | bytes 192 | tf_op jit(solution)/shard_map/psum | solution.py:148
  (92 shorter events, 45.2 us)
Async XLA Ops:
  0.6 17.3 %copy-start = (f32[2,8,8,16,128]{4,3,2,1,0:T(8,128)S(1)}, f32[2,8,8,16,128]{4,3,2,1,0:T(8,128)}, u32[]{:S(2)}) copy-start(f32[2,8,8,16,128]{4,3,2,1,0:T(8,128)} %param.8) | copy-start | bytes 3145732
  1.7 16.2 %collective-permute-start = (f32[2,8,1,16,128]{4,3,2,1,0:T(8,128)S(1)}, f32[2,8,1,16,128]{4,3,2,1,0:T(8,128)S(1)}, u32[]{:S(2)}, u32[]{:S(2)}) collective-permute-start(f32[2,8,1,16,128]{4,3,2,1,0:T(8,128)S(1)} %get-tuple-element.31), channel_id=1, source_target_pairs={{0,32},{32,64},{64,96},{96,128},{128,160},{160,192},{192,224},{1,3... | collective-permute-start | bytes 393224 | tf_op jit(solution)/shard_map/ppermute | solution.py:20
  6.2 11.8 %collective-permute-start.1 = (f32[2,8,1,16,128]{4,3,2,1,0:T(8,128)S(1)}, f32[2,8,1,16,128]{4,3,2,1,0:T(8,128)S(1)}, u32[]{:S(2)}, u32[]{:S(2)}) collective-permute-start(f32[2,8,1,16,128]{4,3,2,1,0:T(8,128)S(1)} %get-tuple-element.30), channel_id=1, source_target_pairs={{32,0},{64,32},{96,64},{128,96},{160,128},{192,160},{224,192},{33,... | collective-permute-start | bytes 393224 | tf_op jit(solution)/shard_map/ppermute | solution.py:23
  18.2 5.0 %collective-permute-start.2 = (f32[2,8,10,1,128]{4,3,2,1,0:T(1,128)S(1)}, f32[2,8,10,1,128]{4,3,2,1,0:T(1,128)S(1)}, u32[]{:S(2)}, u32[]{:S(2)}) collective-permute-start(f32[2,8,10,1,128]{4,3,2,1,0:T(1,128)S(1)} %get-tuple-element.22), channel_id=1, source_target_pairs={{0,1},{1,2},{2,3},{3,4},{4,5},{5,6},{6,7},{7,8},{8,9},{9,10},{10,1... | collective-permute-start | bytes 245768 | tf_op jit(solution)/shard_map/ppermute | solution.py:20
  21.8 5.4 %collective-permute-start.3 = (f32[2,8,10,1,128]{4,3,2,1,0:T(1,128)S(1)}, f32[2,8,10,1,128]{4,3,2,1,0:T(1,128)S(1)}, u32[]{:S(2)}, u32[]{:S(2)}) collective-permute-start(f32[2,8,10,1,128]{4,3,2,1,0:T(1,128)S(1)} %get-tuple-element.23), channel_id=1, source_target_pairs={{1,0},{2,1},{3,2},{4,3},{5,4},{6,5},{7,6},{8,7},{9,8},{10,9},{11,1... | collective-permute-start | bytes 245768 | tf_op jit(solution)/shard_map/ppermute | solution.py:23
  23.2 3.9 %copy-start.6 = (f32[2,8,10,1,128]{4,3,2,1,0:T(1,128)}, f32[2,8,10,1,128]{4,3,2,1,0:T(1,128)S(1)}, u32[]{:S(2)}) copy-start(f32[2,8,10,1,128]{4,3,2,1,0:T(1,128)S(1)} %collective-permute-done.2) | copy-start | bytes 245764
  27.1 0.6 copy-start.7
  29.5 5.7 %copy-start.3 = (f32[8,16,128]{2,1,0:T(8,128)S(1)}, f32[8,16,128]{2,1,0:T(8,128)}, u32[]{:S(2)}) copy-start(f32[8,16,128]{2,1,0:T(8,128)} %param.11) | copy-start | bytes 196612
  29.5 5.7 %copy-start.4 = (f32[8,16,128]{2,1,0:T(8,128)S(1)}, f32[8,16,128]{2,1,0:T(8,128)}, u32[]{:S(2)}) copy-start(f32[8,16,128]{2,1,0:T(8,128)} %param.10) | copy-start | bytes 196612
  35.2 1.5 copy-start.5
  87.1 2.9 copy-start.8
  94.9 45.4 %all-to-all-start = ((f32[256,1,512]{2,1,0:T(1,128)}), f32[256,1,512]{2,1,0:T(1,128)S(1)}, u32[]{:S(2)}, u32[]{:S(2)}) async-start(f32[256,1,512]{2,1,0:T(1,128)} %reshape.278), calls=%async_computation | async-start | bytes 1048576 | tf_op jit(solution)/shard_map/all_to_all | solution.py:11
  149.8 4.5 %copy-start.1 = (f32[2,32,8192]{2,1,0:T(8,128)S(1)}, f32[2,32,8192]{2,1,0:T(8,128)}, u32[]{:S(2)}) copy-start(f32[2,32,8192]{2,1,0:T(8,128)} %param.12) | copy-start | bytes 6291460
  201.4 1.1 copy-start.2
  202.6 16.4 %collective-permute-start.4 = (f32[2,8,1,16,128]{4,3,2,1,0:T(8,128)S(1)}, f32[2,8,1,16,128]{4,3,2,1,0:T(8,128)S(1)}, u32[]{:S(2)}, u32[]{:S(2)}) collective-permute-start(f32[2,8,1,16,128]{4,3,2,1,0:T(8,128)S(1)} %get-tuple-element.28), channel_id=1, source_target_pairs={{0,32},{32,64},{64,96},{96,128},{128,160},{160,192},{192,224},{1,3... | collective-permute-start | bytes 393224 | tf_op jit(solution)/shard_map/ppermute | solution.py:20
  217.1 6.3 %collective-permute-start.5 = (f32[2,8,1,16,128]{4,3,2,1,0:T(8,128)S(1)}, f32[2,8,1,16,128]{4,3,2,1,0:T(8,128)S(1)}, u32[]{:S(2)}, u32[]{:S(2)}) collective-permute-start(f32[2,8,1,16,128]{4,3,2,1,0:T(8,128)S(1)} %get-tuple-element.29), channel_id=1, source_target_pairs={{32,0},{64,32},{96,64},{128,96},{160,128},{192,160},{224,192},{33,... | collective-permute-start | bytes 393224 | tf_op jit(solution)/shard_map/ppermute | solution.py:23
  223.5 4.6 %collective-permute-start.6 = (f32[2,8,10,1,128]{4,3,2,1,0:T(1,128)S(1)}, f32[2,8,10,1,128]{4,3,2,1,0:T(1,128)S(1)}, u32[]{:S(2)}, u32[]{:S(2)}) collective-permute-start(f32[2,8,10,1,128]{4,3,2,1,0:T(1,128)S(1)} %get-tuple-element.20), channel_id=1, source_target_pairs={{0,1},{1,2},{2,3},{3,4},{4,5},{5,6},{6,7},{7,8},{8,9},{9,10},{10,1... | collective-permute-start | bytes 245768 | tf_op jit(solution)/shard_map/ppermute | solution.py:20
  226.6 5.2 %collective-permute-start.7 = (f32[2,8,10,1,128]{4,3,2,1,0:T(1,128)S(1)}, f32[2,8,10,1,128]{4,3,2,1,0:T(1,128)S(1)}, u32[]{:S(2)}, u32[]{:S(2)}) collective-permute-start(f32[2,8,10,1,128]{4,3,2,1,0:T(1,128)S(1)} %get-tuple-element.21), channel_id=1, source_target_pairs={{1,0},{2,1},{3,2},{4,3},{5,4},{6,5},{7,6},{8,7},{9,8},{10,9},{11,1... | collective-permute-start | bytes 245768 | tf_op jit(solution)/shard_map/ppermute | solution.py:23
